TPU v7x, 256 devices: a whole 4x4x8 slice. The times are simulated.
256 devices in a mesh: row: 16 (over y, z_lo, core), col: 16 (over z_hi, x).
Axes of the slice: x: 4, y: 4, z: 8 (z_hi: 4, z_lo: 2; z = z_hi * 2 + z_lo), core: 2. Of those that a mesh axis runs over, the one named last changes fastest.
Arguments:
- features: bfloat16 [131072, 256], P(('row', 'col')), may hold values from -6 to 6
- w_self: bfloat16 [256, 256], replicated, may hold values from -0.375 to 0.375
- w_neigh: bfloat16 [256, 256], replicated, may hold values from -3 to 3
- cotangent: bfloat16 [131072, 256], P(('row', 'col')), may hold values from -6 to 6
- degree: int32 [131072], P(('row', 'col')), may hold values from 64 to 256
- tile_rows: int32 [65536], P(('row', 'col')), may hold values from 0 to 63
- tile_cols: int32 [65536], P(('row', 'col')), may hold values from 0 to 63
- tile_edges: int32 [4, 65536, 128], P(None, ('row', 'col')), may hold values from 0 to 127
- tile_count: int32 [256], P(('row', 'col')), may hold values from 4 to 256, as said below
Outputs:
- activations: bfloat16 [131072, 256], P(('row', 'col'))
- feature_grad: bfloat16 [131072, 256], P(('row', 'col'))
- grad_self: float32 [256, 256], replicated
- grad_neigh: float32 [256, 256], replicated
Inputs may be any that keep to these rules, and one draw needn't show every extreme that they name: The busiest device uses all 256 of its slots; slots from tile_count on are ignored.
All inputs are finite; a program needn't handle non-finite values.
Results may differ from a plain program's by a relative error of at most 0.0059.
Values may be sent and summed in bfloat16 or wider, within the bound.
No kernel may reach another device: no remote copies, remote signals or barrier semaphores. Data moves between devices by JAX's collectives and lax.ppermute only.
A program may use at most 64 MiB of HBM per device.

v0:
```python
import math
import jax
import jax.numpy as jnp
from jax import lax
from jax.sharding import PartitionSpec as P


def tile_masks(edges_here, use_here):
    tile_size = edges_here.shape[2]
    matches = edges_here[:, :, :, None] == jnp.arange(tile_size, dtype=jnp.int32)
    multiplicity = jnp.sum(matches.astype(jnp.float32), axis=0)
    return (multiplicity * use_here[:, None, None]).astype(jnp.bfloat16)


def sum_weights(part_self, part_neigh):
    return lax.psum((part_self, part_neigh), ("row", "col"))


def spread_back(dscaled, row_blocks, col_blocks, edge_blocks, use_blocks, col_tile_count):
    tile_size = edge_blocks.shape[3]
    feature_dim = dscaled.shape[1]
    row_nodes = lax.all_gather(dscaled, "col", axis=0, tiled=True)
    row_tiles = row_nodes.reshape(-1, tile_size, feature_dim)

    def backward_round(running, inputs):
        rows_here, cols_here, edges_here, use_here = inputs
        pattern = tile_masks(edges_here, use_here)
        contribution = jnp.einsum(
            "bqc,bqf->bcf", pattern, row_tiles[rows_here], preferred_element_type=jnp.float32
        )
        return (running.at[cols_here].add(contribution), None)

    start_value = jnp.zeros((col_tile_count, tile_size, feature_dim), jnp.float32)
    partial_grads, _ = lax.scan(
        backward_round, start_value, (row_blocks, col_blocks, edge_blocks, use_blocks)
    )
    return lax.psum_scatter(
        partial_grads.reshape(-1, feature_dim), "row", scatter_dimension=0, tiled=True
    )


def per_device(
    features, w_self, w_neigh, cotangent, degree, tile_rows, tile_cols, tile_edges, tile_count
):
    local_rows, feature_dim = features.shape
    tile_size = tile_edges.shape[2]
    slot_count = tile_rows.shape[0]
    row_devices = lax.axis_size("row")
    col_devices = lax.axis_size("col")
    in_use = (jnp.arange(slot_count, dtype=jnp.int32) < tile_count[0]).astype(jnp.float32)
    block_size = math.gcd(slot_count, 32)
    rounds = slot_count // block_size
    edge_blocks = tile_edges.reshape(tile_edges.shape[0], rounds, block_size, tile_size).transpose(
        1, 0, 2, 3
    )
    row_blocks = tile_rows.reshape(rounds, block_size)
    col_blocks = tile_cols.reshape(rounds, block_size)
    use_blocks = in_use.reshape(rounds, block_size)
    row_tile_count = local_rows * col_devices // tile_size
    col_tile_count = local_rows * row_devices // tile_size
    column_nodes = lax.all_gather(features, "row", axis=0, tiled=True)
    column_tiles = column_nodes.reshape(-1, tile_size, feature_dim)

    def forward_round(running, inputs):
        rows_here, cols_here, edges_here, use_here = inputs
        pattern = tile_masks(edges_here, use_here)
        product = jnp.einsum(
            "bqc,bcf->bqf", pattern, column_tiles[cols_here], preferred_element_type=jnp.float32
        )
        return (running.at[rows_here].add(product), None)

    start_value = jnp.zeros((row_tile_count, tile_size, feature_dim), jnp.float32)
    partial_sums, _ = lax.scan(
        forward_round, start_value, (row_blocks, col_blocks, edge_blocks, use_blocks)
    )
    neighbour_sum = lax.psum_scatter(
        partial_sums.reshape(-1, feature_dim), "col", scatter_dimension=0, tiled=True
    )
    degree_wide = degree.astype(jnp.float32)[:, None]
    aggregate = (neighbour_sum / degree_wide).astype(jnp.bfloat16)
    preact = jnp.dot(features, w_self, preferred_element_type=jnp.float32) + jnp.dot(
        aggregate, w_neigh, preferred_element_type=jnp.float32
    )
    sigmoid_pre = jax.nn.sigmoid(preact)
    activations = (preact * sigmoid_pre).astype(jnp.bfloat16)
    slope = sigmoid_pre * (1.0 + preact * (1.0 - sigmoid_pre))
    dpreact = (cotangent.astype(jnp.float32) * slope).astype(jnp.bfloat16)
    part_self = jnp.einsum("nf,ng->fg", features, dpreact, preferred_element_type=jnp.float32)
    part_neigh = jnp.einsum("nf,ng->fg", aggregate, dpreact, preferred_element_type=jnp.float32)
    dscaled = (
        jnp.einsum("ng,fg->nf", dpreact, w_neigh, preferred_element_type=jnp.float32) / degree_wide
    ).astype(jnp.bfloat16)
    neighbour_grad = spread_back(
        dscaled, row_blocks, col_blocks, edge_blocks, use_blocks, col_tile_count
    )
    grad_pair = sum_weights(part_self, part_neigh)
    own_grad = jnp.einsum("ng,fg->nf", dpreact, w_self, preferred_element_type=jnp.float32)
    feature_grad = (own_grad + neighbour_grad).astype(jnp.bfloat16)
    total_nodes = local_rows * row_devices * col_devices
    grad_scale = 1.0 / math.sqrt(total_nodes)
    return (activations, feature_grad, grad_pair[0] * grad_scale, grad_pair[1] * grad_scale)


def solution(mesh):
    return jax.shard_map(
        per_device,
        mesh=mesh,
        in_specs=(
            P(("row", "col"), None),
            P(),
            P(),
            P(("row", "col"), None),
            P(("row", "col")),
            P(("row", "col")),
            P(("row", "col")),
            P(None, ("row", "col"), None),
            P(("row", "col")),
        ),
        out_specs=(P(("row", "col"), None), P(("row", "col"), None), P(), P()),
        check_vma=False,
    )
```

profile of v0, /device:TPU:2, one launch (start us, length us, event | category | flops | bytes accessed | tf_op | source)
XLA Modules:
  0.0 771.7 jit_solution(11886097251280555593)
XLA Ops:
  11.2 41.7 %all-gather.3.cloned.1.call-done = bf16[8192,256]{1,0:T(8,128)(2,1)} async-done(((bf16[512,256]{1,0:T(8,128)(2,1)}), bf16[8192,256]{1,0:T(8,128)(2,1)}) %all-gather.3.cloned.1.call-update) | async-done | bytes 4194320 | tf_op jit(solution)/shard_map/all_gather | solution.py:61
  52.9 4.3 broadcast.81.clone
  57.1 147.1 %while.20 = (s32[]{:T(128)}, f32[64,128,256]{2,1,0:T(8,128)}, s32[8,32]{1,0:T(8,128)S(1)}, s32[8,4,32,128]{3,2,1,0:T(8,128)S(1)}, f32[8,32]{1,0:T(8,128)S(1)}, /...) while((s32[]{:T(128)}, f32[64,128,256]{2,1,0:T(8,128)}, s32[8,32]{1,0:T(8,128)S(1)}, ...), condition=%wide.region_3.4_spmd, body=%wide.region_0.3_spmd.sunk | while | flops 276300992 | bytes 27465064 | solution.py:73
  65.7 9.8 %scatter_fusion = f32[64,128,256]{2,1,0:T(8,128)} fusion(f32[64,128,256]{2,1,0:T(8,128)} %get-tuple-element.261, s32[32]{0:T(128)S(1)} %get-tuple-element.241, f32[32,128,256]{2,1,0:T(8,128)} %fusion.44), kind=kCustom, calls=%fused_computation.2.clone.1 | custom fusion | flops 1048576 | bytes 12583040 | tf_op jit(solution)/shard_map/while/body/eval_jaxpr/scatter-add | solution.py:70
  84.2 9.7 %scatter_fusion = f32[64,128,256]{2,1,0:T(8,128)} fusion(f32[64,128,256]{2,1,0:T(8,128)} %get-tuple-element.261, s32[32]{0:T(128)S(1)} %get-tuple-element.241, f32[32,128,256]{2,1,0:T(8,128)} %fusion.44), kind=kCustom, calls=%fused_computation.2.clone.1 | custom fusion | flops 1048576 | bytes 12583040 | tf_op jit(solution)/shard_map/while/body/eval_jaxpr/scatter-add | solution.py:70
  102.4 9.7 %scatter_fusion = f32[64,128,256]{2,1,0:T(8,128)} fusion(f32[64,128,256]{2,1,0:T(8,128)} %get-tuple-element.261, s32[32]{0:T(128)S(1)} %get-tuple-element.241, f32[32,128,256]{2,1,0:T(8,128)} %fusion.44), kind=kCustom, calls=%fused_computation.2.clone.1 | custom fusion | flops 1048576 | bytes 12583040 | tf_op jit(solution)/shard_map/while/body/eval_jaxpr/scatter-add | solution.py:70
  120.7 9.6 %scatter_fusion = f32[64,128,256]{2,1,0:T(8,128)} fusion(f32[64,128,256]{2,1,0:T(8,128)} %get-tuple-element.261, s32[32]{0:T(128)S(1)} %get-tuple-element.241, f32[32,128,256]{2,1,0:T(8,128)} %fusion.44), kind=kCustom, calls=%fused_computation.2.clone.1 | custom fusion | flops 1048576 | bytes 12583040 | tf_op jit(solution)/shard_map/while/body/eval_jaxpr/scatter-add | solution.py:70
  139.0 9.8 %scatter_fusion = f32[64,128,256]{2,1,0:T(8,128)} fusion(f32[64,128,256]{2,1,0:T(8,128)} %get-tuple-element.261, s32[32]{0:T(128)S(1)} %get-tuple-element.241, f32[32,128,256]{2,1,0:T(8,128)} %fusion.44), kind=kCustom, calls=%fused_computation.2.clone.1 | custom fusion | flops 1048576 | bytes 12583040 | tf_op jit(solution)/shard_map/while/body/eval_jaxpr/scatter-add | solution.py:70
  157.3 9.8 %scatter_fusion = f32[64,128,256]{2,1,0:T(8,128)} fusion(f32[64,128,256]{2,1,0:T(8,128)} %get-tuple-element.261, s32[32]{0:T(128)S(1)} %get-tuple-element.241, f32[32,128,256]{2,1,0:T(8,128)} %fusion.44), kind=kCustom, calls=%fused_computation.2.clone.1 | custom fusion | flops 1048576 | bytes 12583040 | tf_op jit(solution)/shard_map/while/body/eval_jaxpr/scatter-add | solution.py:70
  175.7 9.9 %scatter_fusion = f32[64,128,256]{2,1,0:T(8,128)} fusion(f32[64,128,256]{2,1,0:T(8,128)} %get-tuple-element.261, s32[32]{0:T(128)S(1)} %get-tuple-element.241, f32[32,128,256]{2,1,0:T(8,128)} %fusion.44), kind=kCustom, calls=%fused_computation.2.clone.1 | custom fusion | flops 1048576 | bytes 12583040 | tf_op jit(solution)/shard_map/while/body/eval_jaxpr/scatter-add | solution.py:70
  194.2 10.0 %scatter_fusion = f32[64,128,256]{2,1,0:T(8,128)} fusion(f32[64,128,256]{2,1,0:T(8,128)} %get-tuple-element.261, s32[32]{0:T(128)S(1)} %get-tuple-element.241, f32[32,128,256]{2,1,0:T(8,128)} %fusion.44), kind=kCustom, calls=%fused_computation.2.clone.1 | custom fusion | flops 1048576 | bytes 12583040 | tf_op jit(solution)/shard_map/while/body/eval_jaxpr/scatter-add | solution.py:70
  205.4 119.9 %reduce-scatter.3.cloned.1.call-done = f32[512,256]{1,0:T(8,128)} async-done(((f32[8192,256]{1,0:T(8,128)}), f32[512,256]{1,0:T(8,128)}) %reduce-scatter.3.cloned.1.call-update) | async-done | bytes 524304 | tf_op jit(solution)/shard_map/reduce_scatter | solution.py:76
  330.7 72.7 %all-gather.5.cloned.1.call-done = bf16[8192,256]{1,0:T(8,128)(2,1)} async-done(((bf16[512,256]{1,0:T(8,128)(2,1)}), bf16[8192,256]{1,0:T(8,128)(2,1)}) %all-gather.5.cloned.1.call-update) | async-done | bytes 4194320 | tf_op jit(solution)/shard_map/all_gather | solution.py:22
  407.6 150.2 %while.21 = (s32[]{:T(128)}, f32[64,128,256]{2,1,0:T(8,128)}, s32[8,32]{1,0:T(8,128)S(1)}, s32[8,4,32,128]{3,2,1,0:T(8,128)S(1)}, f32[8,32]{1,0:T(8,128)S(1)}, /...) while((s32[]{:T(128)}, f32[64,128,256]{2,1,0:T(8,128)}, s32[8,32]{1,0:T(8,128)S(1)}, ...), condition=%wide.region_8.9_spmd, body=%wide.region_5.8_spmd.sunk | while | flops 276300992 | bytes 27465064 | solution.py:34
  416.4 9.9 %scatter_fusion.1 = f32[64,128,256]{2,1,0:T(8,128)} fusion(f32[64,128,256]{2,1,0:T(8,128)} %get-tuple-element.285, s32[32]{0:T(128)S(1)} %get-tuple-element.250, f32[32,128,256]{2,1,0:T(8,128)} %fusion.48), kind=kCustom, calls=%fused_computation.3.clone.1 | custom fusion | flops 1048576 | bytes 12583040 | tf_op jit(solution)/shard_map/while/body/eval_jaxpr/scatter-add | solution.py:31
  435.1 10.1 %scatter_fusion.1 = f32[64,128,256]{2,1,0:T(8,128)} fusion(f32[64,128,256]{2,1,0:T(8,128)} %get-tuple-element.285, s32[32]{0:T(128)S(1)} %get-tuple-element.250, f32[32,128,256]{2,1,0:T(8,128)} %fusion.48), kind=kCustom, calls=%fused_computation.3.clone.1 | custom fusion | flops 1048576 | bytes 12583040 | tf_op jit(solution)/shard_map/while/body/eval_jaxpr/scatter-add | solution.py:31
  453.9 10.0 %scatter_fusion.1 = f32[64,128,256]{2,1,0:T(8,128)} fusion(f32[64,128,256]{2,1,0:T(8,128)} %get-tuple-element.285, s32[32]{0:T(128)S(1)} %get-tuple-element.250, f32[32,128,256]{2,1,0:T(8,128)} %fusion.48), kind=kCustom, calls=%fused_computation.3.clone.1 | custom fusion | flops 1048576 | bytes 12583040 | tf_op jit(solution)/shard_map/while/body/eval_jaxpr/scatter-add | solution.py:31
  472.7 10.0 %scatter_fusion.1 = f32[64,128,256]{2,1,0:T(8,128)} fusion(f32[64,128,256]{2,1,0:T(8,128)} %get-tuple-element.285, s32[32]{0:T(128)S(1)} %get-tuple-element.250, f32[32,128,256]{2,1,0:T(8,128)} %fusion.48), kind=kCustom, calls=%fused_computation.3.clone.1 | custom fusion | flops 1048576 | bytes 12583040 | tf_op jit(solution)/shard_map/while/body/eval_jaxpr/scatter-add | solution.py:31
  491.5 10.1 %scatter_fusion.1 = f32[64,128,256]{2,1,0:T(8,128)} fusion(f32[64,128,256]{2,1,0:T(8,128)} %get-tuple-element.285, s32[32]{0:T(128)S(1)} %get-tuple-element.250, f32[32,128,256]{2,1,0:T(8,128)} %fusion.48), kind=kCustom, calls=%fused_computation.3.clone.1 | custom fusion | flops 1048576 | bytes 12583040 | tf_op jit(solution)/shard_map/while/body/eval_jaxpr/scatter-add | solution.py:31
  510.4 10.1 %scatter_fusion.1 = f32[64,128,256]{2,1,0:T(8,128)} fusion(f32[64,128,256]{2,1,0:T(8,128)} %get-tuple-element.285, s32[32]{0:T(128)S(1)} %get-tuple-element.250, f32[32,128,256]{2,1,0:T(8,128)} %fusion.48), kind=kCustom, calls=%fused_computation.3.clone.1 | custom fusion | flops 1048576 | bytes 12583040 | tf_op jit(solution)/shard_map/while/body/eval_jaxpr/scatter-add | solution.py:31
  529.2 9.9 %scatter_fusion.1 = f32[64,128,256]{2,1,0:T(8,128)} fusion(f32[64,128,256]{2,1,0:T(8,128)} %get-tuple-element.285, s32[32]{0:T(128)S(1)} %get-tuple-element.250, f32[32,128,256]{2,1,0:T(8,128)} %fusion.48), kind=kCustom, calls=%fused_computation.3.clone.1 | custom fusion | flops 1048576 | bytes 12583040 | tf_op jit(solution)/shard_map/while/body/eval_jaxpr/scatter-add | solution.py:31
  547.9 10.0 %scatter_fusion.1 = f32[64,128,256]{2,1,0:T(8,128)} fusion(f32[64,128,256]{2,1,0:T(8,128)} %get-tuple-element.285, s32[32]{0:T(128)S(1)} %get-tuple-element.250, f32[32,128,256]{2,1,0:T(8,128)} %fusion.48), kind=kCustom, calls=%fused_computation.3.clone.1 | custom fusion | flops 1048576 | bytes 12583040 | tf_op jit(solution)/shard_map/while/body/eval_jaxpr/scatter-add | solution.py:31
  557.9 103.7 %all-reduce.3.cloned.1.call-done = (f32[256,256]{0,1:T(8,128)}, f32[256,256]{0,1:T(8,128)}) async-done(((f32[256,256]{0,1:T(8,128)}, f32[256,256]{0,1:T(8,128)}), (f32[256,256]{0,1:T(8,128)}, f32[256,256]{0,1:T(8,128)})) %all-reduce.3.cloned.1.call-update) | async-done | bytes 524304 | tf_op jit(solution)/shard_map/psum | solution.py:16
  664.4 98.7 %reduce-scatter.5.cloned.1.call-done = f32[512,256]{1,0:T(8,128)} async-done(((f32[8192,256]{1,0:T(8,128)}), f32[512,256]{1,0:T(8,128)}) %reduce-scatter.5.cloned.1.call-update) | async-done | bytes 524304 | tf_op jit(solution)/shard_map/reduce_scatter | solution.py:37
  (148 shorter events, 157.3 us)
Async XLA Ops:
  7.2 319.3 %copy-start = (bf16[256,256]{1,0:T(8,128)(2,1)S(1)}, bf16[256,256]{1,0:T(8,128)(2,1)}, u32[]{:S(2)}) copy-start(bf16[256,256]{1,0:T(8,128)(2,1)} %param.15) | copy-start | bytes 393220
  7.2 45.7 %all-gather.3.cloned.1.call-start = ((), (), s32[]{:S(2)}) async-start(), calls=%async_computation.2 | async-start | bytes 4456448 | tf_op jit(solution)/shard_map/all_gather | solution.py:61
  7.9 317.4 %reduce-scatter.3.cloned.1.call-start = ((), (), s32[]{:S(2)}) async-start(), calls=%async_computation.3 | async-start | bytes 8912896 | tf_op jit(solution)/shard_map/reduce_scatter | solution.py:76
  204.2 0.7 copy-start.3
  204.2 1.0 copy-start.1
  204.2 1.0 copy-start.2
  204.2 122.3 %copy-start.4 = (bf16[512,256]{1,0:T(8,128)(2,1)S(1)}, bf16[512,256]{1,0:T(8,128)(2,1)}, u32[]{:S(2)}) copy-start(bf16[512,256]{1,0:T(8,128)(2,1)} %param.16) | copy-start | bytes 786436
  204.2 199.1 %all-gather.5.cloned.1.call-start = ((), (), s32[]{:S(2)}) async-start(), calls=%async_computation.4 | async-start | bytes 4456448 | tf_op jit(solution)/shard_map/all_gather | solution.py:22
  328.6 333.0 %all-reduce.3.cloned.1.call-start = ((), (), s32[]{:S(2)}) async-start(), calls=%async_computation.6 | async-start | bytes 1048576 | tf_op jit(solution)/shard_map/psum | solution.py:16
  330.6 432.5 %reduce-scatter.5.cloned.1.call-start = ((), (), s32[]{:S(2)}) async-start(), calls=%async_computation.5 | async-start | bytes 8912896 | tf_op jit(solution)/shard_map/reduce_scatter | solution.py:37
Sparse Core Ops, SparseCore 0:
  9.9 42.9 all-gather.2
  204.4 120.8 reduce-scatter.2
  328.7 74.6 all-gather.4
  409.4 252.1 all-reduce.2
  664.0 99.0 reduce-scatter.4
where the time goes:
time: 773 us; the launch traced here: 772 us
  waiting for transfers between devices  437 us (57%)
  other arithmetic  208 us (27%)
  local copies, waits for them, and re-layouts  60 us (8%)
  matrix products  51.1 us (7%)
  between operations  14.5 us (2%)
    reduce_scatter x1, waiting for transfers between devices, per_device(): lax.psum_scatter(partial_sums.reshape(-1, feature_dim), 'col', scatter_di...  120 us
    psum x1, waiting for transfers between devices, sum_weights(): return lax.psum((part_self, part_neigh), ('row', 'col'))  104 us
    reduce_scatter x1, waiting for transfers between devices, spread_back(): lax.psum_scatter(partial_grads.reshape(-1, feature_dim), 'row', scatter_d...  98.7 us
    scatter-add x8, other arithmetic, backward_round(): return (running.at[cols_here].add(contribution), None)  80.1 us
    scatter-add x8, other arithmetic, forward_round(): return (running.at[rows_here].add(product), None)  78.3 us
    all_gather x1, waiting for transfers between devices, spread_back(): row_nodes = lax.all_gather(dscaled, 'col', axis=0, tiled=True)  72.7 us
    reduce_sum x16, other arithmetic, tile_masks(): multiplicity = jnp.sum(matches.astype(jnp.float32), axis=0)  46.9 us
    all_gather x1, waiting for transfers between devices, per_device(): column_nodes = lax.all_gather(features, 'row', axis=0, tiled=True)  41.7 us
  transfers between devices with their start and end apart: 5, of which 5 were waited for; matrix products, arithmetic and copies ran while one was open for 21% of the time, Pallas kernels for 0%

commit v1 on v0

--- a/solution.py
+++ b/solution.py
@@ -13,7 +13,7 @@
 
 
 def sum_weights(part_self, part_neigh):
-    return lax.psum((part_self, part_neigh), ("row", "col"))
+    return lax.psum(lax.psum((part_self, part_neigh), "col"), "row")
 
 
 def spread_back(dscaled, row_blocks, col_blocks, edge_blocks, use_blocks, col_tile_count):

time: 773 us -> 837 us (1.083)
  waiting for transfers between devices: 437 us -> 502 us
    psum x1 -> x2, waiting for transfers between devices: 104 us -> 164 us  [sum_weights(): return lax.psum(lax.psum((part_self, part_neigh), 'col'), 'row')]
  transfers between devices with their start and end apart: 5 -> 6, of which waited for: 5 -> 5; matrix products, arithmetic and copies ran while one was open for 21% -> 19% of each run, Pallas kernels for 0% -> 0%
where the time goes in v1:
time: 837 us; the launch traced here: 836 us
  waiting for transfers between devices  502 us (60%)
  other arithmetic  208 us (25%)
  local copies, waits for them, and re-layouts  60 us (7%)
  matrix products  51 us (6%)
  between operations  14.8 us (2%)
    psum x2, waiting for transfers between devices, sum_weights(): return lax.psum(lax.psum((part_self, part_neigh), 'col'), 'row')  164 us
    reduce_scatter x1, waiting for transfers between devices, per_device(): lax.psum_scatter(partial_sums.reshape(-1, feature_dim), 'col', scatter_di...  120 us
    reduce_scatter x1, waiting for transfers between devices, spread_back(): lax.psum_scatter(partial_grads.reshape(-1, feature_dim), 'row', scatter_d...  97.6 us
    scatter-add x8, other arithmetic, backward_round(): return (running.at[cols_here].add(contribution), None)  80.1 us
    scatter-add x8, other arithmetic, forward_round(): return (running.at[rows_here].add(product), None)  78.2 us
    all_gather x1, waiting for transfers between devices, spread_back(): row_nodes = lax.all_gather(dscaled, 'col', axis=0, tiled=True)  78 us
    reduce_sum x16, other arithmetic, tile_masks(): multiplicity = jnp.sum(matches.astype(jnp.float32), axis=0)  46.9 us
    all_gather x1, waiting for transfers between devices, per_device(): column_nodes = lax.all_gather(features, 'row', axis=0, tiled=True)  41.7 us
  transfers between devices with their start and end apart: 6, of which 5 were waited for; matrix products, arithmetic and copies ran while one was open for 19% of the time, Pallas kernels for 0%

profile of v1, /device:TPU:2, one launch (start us, length us, event | category | flops | bytes accessed | tf_op | source)
XLA Modules:
  0.0 835.8 jit_solution(13679926930401774520)
XLA Ops:
  11.2 41.7 %all-gather.3.cloned.1.call-done = bf16[8192,256]{1,0:T(8,128)(2,1)} async-done(((bf16[512,256]{1,0:T(8,128)(2,1)}), bf16[8192,256]{1,0:T(8,128)(2,1)}) %all-gather.3.cloned.1.call-update) | async-done | bytes 4194320 | tf_op jit(solution)/shard_map/all_gather | solution.py:61
  52.9 4.3 broadcast.81.clone
  57.1 146.8 %while.20 = (s32[]{:T(128)}, f32[64,128,256]{2,1,0:T(8,128)}, s32[8,32]{1,0:T(8,128)S(1)}, s32[8,4,32,128]{3,2,1,0:T(8,128)S(1)}, f32[8,32]{1,0:T(8,128)S(1)}, /...) while((s32[]{:T(128)}, f32[64,128,256]{2,1,0:T(8,128)}, s32[8,32]{1,0:T(8,128)S(1)}, ...), condition=%wide.region_3.4_spmd, body=%wide.region_0.3_spmd.sunk | while | flops 276300992 | bytes 27465064 | solution.py:73
  65.7 9.8 %scatter_fusion = f32[64,128,256]{2,1,0:T(8,128)} fusion(f32[64,128,256]{2,1,0:T(8,128)} %get-tuple-element.263, s32[32]{0:T(128)S(1)} %get-tuple-element.243, f32[32,128,256]{2,1,0:T(8,128)} %fusion.44), kind=kCustom, calls=%fused_computation.2.clone.1 | custom fusion | flops 1048576 | bytes 12583040 | tf_op jit(solution)/shard_map/while/body/eval_jaxpr/scatter-add | solution.py:70
  84.1 9.7 %scatter_fusion = f32[64,128,256]{2,1,0:T(8,128)} fusion(f32[64,128,256]{2,1,0:T(8,128)} %get-tuple-element.263, s32[32]{0:T(128)S(1)} %get-tuple-element.243, f32[32,128,256]{2,1,0:T(8,128)} %fusion.44), kind=kCustom, calls=%fused_computation.2.clone.1 | custom fusion | flops 1048576 | bytes 12583040 | tf_op jit(solution)/shard_map/while/body/eval_jaxpr/scatter-add | solution.py:70
  102.4 9.7 %scatter_fusion = f32[64,128,256]{2,1,0:T(8,128)} fusion(f32[64,128,256]{2,1,0:T(8,128)} %get-tuple-element.263, s32[32]{0:T(128)S(1)} %get-tuple-element.243, f32[32,128,256]{2,1,0:T(8,128)} %fusion.44), kind=kCustom, calls=%fused_computation.2.clone.1 | custom fusion | flops 1048576 | bytes 12583040 | tf_op jit(solution)/shard_map/while/body/eval_jaxpr/scatter-add | solution.py:70
  120.7 9.7 %scatter_fusion = f32[64,128,256]{2,1,0:T(8,128)} fusion(f32[64,128,256]{2,1,0:T(8,128)} %get-tuple-element.263, s32[32]{0:T(128)S(1)} %get-tuple-element.243, f32[32,128,256]{2,1,0:T(8,128)} %fusion.44), kind=kCustom, calls=%fused_computation.2.clone.1 | custom fusion | flops 1048576 | bytes 12583040 | tf_op jit(solution)/shard_map/while/body/eval_jaxpr/scatter-add | solution.py:70
  139.0 9.7 %scatter_fusion = f32[64,128,256]{2,1,0:T(8,128)} fusion(f32[64,128,256]{2,1,0:T(8,128)} %get-tuple-element.263, s32[32]{0:T(128)S(1)} %get-tuple-element.243, f32[32,128,256]{2,1,0:T(8,128)} %fusion.44), kind=kCustom, calls=%fused_computation.2.clone.1 | custom fusion | flops 1048576 | bytes 12583040 | tf_op jit(solution)/shard_map/while/body/eval_jaxpr/scatter-add | solution.py:70
  157.2 9.8 %scatter_fusion = f32[64,128,256]{2,1,0:T(8,128)} fusion(f32[64,128,256]{2,1,0:T(8,128)} %get-tuple-element.263, s32[32]{0:T(128)S(1)} %get-tuple-element.243, f32[32,128,256]{2,1,0:T(8,128)} %fusion.44), kind=kCustom, calls=%fused_computation.2.clone.1 | custom fusion | flops 1048576 | bytes 12583040 | tf_op jit(solution)/shard_map/while/body/eval_jaxpr/scatter-add | solution.py:70
  175.6 9.8 %scatter_fusion = f32[64,128,256]{2,1,0:T(8,128)} fusion(f32[64,128,256]{2,1,0:T(8,128)} %get-tuple-element.263, s32[32]{0:T(128)S(1)} %get-tuple-element.243, f32[32,128,256]{2,1,0:T(8,128)} %fusion.44), kind=kCustom, calls=%fused_computation.2.clone.1 | custom fusion | flops 1048576 | bytes 12583040 | tf_op jit(solution)/shard_map/while/body/eval_jaxpr/scatter-add | solution.py:70
  194.0 10.0 %scatter_fusion = f32[64,128,256]{2,1,0:T(8,128)} fusion(f32[64,128,256]{2,1,0:T(8,128)} %get-tuple-element.263, s32[32]{0:T(128)S(1)} %get-tuple-element.243, f32[32,128,256]{2,1,0:T(8,128)} %fusion.44), kind=kCustom, calls=%fused_computation.2.clone.1 | custom fusion | flops 1048576 | bytes 12583040 | tf_op jit(solution)/shard_map/while/body/eval_jaxpr/scatter-add | solution.py:70
  205.2 119.9 %reduce-scatter.3.cloned.1.call-done = f32[512,256]{1,0:T(8,128)} async-done(((f32[8192,256]{1,0:T(8,128)}), f32[512,256]{1,0:T(8,128)}) %reduce-scatter.3.cloned.1.call-update) | async-done | bytes 524304 | tf_op jit(solution)/shard_map/reduce_scatter | solution.py:76
  330.5 163.5 %all-reduce.5.cloned.1.call-done = (f32[256,256]{0,1:T(8,128)}, f32[256,256]{0,1:T(8,128)}) async-done(((f32[256,256]{0,1:T(8,128)}, f32[256,256]{0,1:T(8,128)}), (f32[256,256]{0,1:T(8,128)}, f32[256,256]{0,1:T(8,128)})) %all-reduce.5.cloned.1.call-update) | async-done | bytes 524304 | tf_op jit(solution)/shard_map/psum | solution.py:16
  494.1 78.0 %all-gather.5.cloned.1.call-done = bf16[8192,256]{1,0:T(8,128)(2,1)} async-done(((bf16[512,256]{1,0:T(8,128)(2,1)}), bf16[8192,256]{1,0:T(8,128)(2,1)}) %all-gather.5.cloned.1.call-update) | async-done | bytes 4194320 | tf_op jit(solution)/shard_map/all_gather | solution.py:22
  576.4 150.1 %while.21 = (s32[]{:T(128)}, f32[64,128,256]{2,1,0:T(8,128)}, s32[8,32]{1,0:T(8,128)S(1)}, s32[8,4,32,128]{3,2,1,0:T(8,128)S(1)}, f32[8,32]{1,0:T(8,128)S(1)}, /...) while((s32[]{:T(128)}, f32[64,128,256]{2,1,0:T(8,128)}, s32[8,32]{1,0:T(8,128)S(1)}, ...), condition=%wide.region_8.9_spmd, body=%wide.region_5.8_spmd.sunk | while | flops 276300992 | bytes 27465064 | solution.py:34
  585.1 9.9 %scatter_fusion.1 = f32[64,128,256]{2,1,0:T(8,128)} fusion(f32[64,128,256]{2,1,0:T(8,128)} %get-tuple-element.287, s32[32]{0:T(128)S(1)} %get-tuple-element.252, f32[32,128,256]{2,1,0:T(8,128)} %fusion.48), kind=kCustom, calls=%fused_computation.3.clone.1 | custom fusion | flops 1048576 | bytes 12583040 | tf_op jit(solution)/shard_map/while/body/eval_jaxpr/scatter-add | solution.py:31
  603.8 10.1 %scatter_fusion.1 = f32[64,128,256]{2,1,0:T(8,128)} fusion(f32[64,128,256]{2,1,0:T(8,128)} %get-tuple-element.287, s32[32]{0:T(128)S(1)} %get-tuple-element.252, f32[32,128,256]{2,1,0:T(8,128)} %fusion.48), kind=kCustom, calls=%fused_computation.3.clone.1 | custom fusion | flops 1048576 | bytes 12583040 | tf_op jit(solution)/shard_map/while/body/eval_jaxpr/scatter-add | solution.py:31
  622.6 10.0 %scatter_fusion.1 = f32[64,128,256]{2,1,0:T(8,128)} fusion(f32[64,128,256]{2,1,0:T(8,128)} %get-tuple-element.287, s32[32]{0:T(128)S(1)} %get-tuple-element.252, f32[32,128,256]{2,1,0:T(8,128)} %fusion.48), kind=kCustom, calls=%fused_computation.3.clone.1 | custom fusion | flops 1048576 | bytes 12583040 | tf_op jit(solution)/shard_map/while/body/eval_jaxpr/scatter-add | solution.py:31
  641.4 10.1 %scatter_fusion.1 = f32[64,128,256]{2,1,0:T(8,128)} fusion(f32[64,128,256]{2,1,0:T(8,128)} %get-tuple-element.287, s32[32]{0:T(128)S(1)} %get-tuple-element.252, f32[32,128,256]{2,1,0:T(8,128)} %fusion.48), kind=kCustom, calls=%fused_computation.3.clone.1 | custom fusion | flops 1048576 | bytes 12583040 | tf_op jit(solution)/shard_map/while/body/eval_jaxpr/scatter-add | solution.py:31
  660.3 10.1 %scatter_fusion.1 = f32[64,128,256]{2,1,0:T(8,128)} fusion(f32[64,128,256]{2,1,0:T(8,128)} %get-tuple-element.287, s32[32]{0:T(128)S(1)} %get-tuple-element.252, f32[32,128,256]{2,1,0:T(8,128)} %fusion.48), kind=kCustom, calls=%fused_computation.3.clone.1 | custom fusion | flops 1048576 | bytes 12583040 | tf_op jit(solution)/shard_map/while/body/eval_jaxpr/scatter-add | solution.py:31
  679.1 10.1 %scatter_fusion.1 = f32[64,128,256]{2,1,0:T(8,128)} fusion(f32[64,128,256]{2,1,0:T(8,128)} %get-tuple-element.287, s32[32]{0:T(128)S(1)} %get-tuple-element.252, f32[32,128,256]{2,1,0:T(8,128)} %fusion.48), kind=kCustom, calls=%fused_computation.3.clone.1 | custom fusion | flops 1048576 | bytes 12583040 | tf_op jit(solution)/shard_map/while/body/eval_jaxpr/scatter-add | solution.py:31
  697.9 9.9 %scatter_fusion.1 = f32[64,128,256]{2,1,0:T(8,128)} fusion(f32[64,128,256]{2,1,0:T(8,128)} %get-tuple-element.287, s32[32]{0:T(128)S(1)} %get-tuple-element.252, f32[32,128,256]{2,1,0:T(8,128)} %fusion.48), kind=kCustom, calls=%fused_computation.3.clone.1 | custom fusion | flops 1048576 | bytes 12583040 | tf_op jit(solution)/shard_map/while/body/eval_jaxpr/scatter-add | solution.py:31
  716.6 9.9 %scatter_fusion.1 = f32[64,128,256]{2,1,0:T(8,128)} fusion(f32[64,128,256]{2,1,0:T(8,128)} %get-tuple-element.287, s32[32]{0:T(128)S(1)} %get-tuple-element.252, f32[32,128,256]{2,1,0:T(8,128)} %fusion.48), kind=kCustom, calls=%fused_computation.3.clone.1 | custom fusion | flops 1048576 | bytes 12583040 | tf_op jit(solution)/shard_map/while/body/eval_jaxpr/scatter-add | solution.py:31
  729.3 97.6 %reduce-scatter.5.cloned.1.call-done = f32[512,256]{1,0:T(8,128)} async-done(((f32[8192,256]{1,0:T(8,128)}), f32[512,256]{1,0:T(8,128)}) %reduce-scatter.5.cloned.1.call-update) | async-done | bytes 524304 | tf_op jit(solution)/shard_map/reduce_scatter | solution.py:37
  (151 shorter events, 157.1 us)
Async XLA Ops:
  7.2 319.2 %copy-start = (bf16[256,256]{1,0:T(8,128)(2,1)S(1)}, bf16[256,256]{1,0:T(8,128)(2,1)}, u32[]{:S(2)}) copy-start(bf16[256,256]{1,0:T(8,128)(2,1)} %param.15) | copy-start | bytes 393220
  7.2 45.7 %all-gather.3.cloned.1.call-start = ((), (), s32[]{:S(2)}) async-start(), calls=%async_computation.2 | async-start | bytes 4456448 | tf_op jit(solution)/shard_map/all_gather | solution.py:61
  7.9 317.2 %reduce-scatter.3.cloned.1.call-start = ((), (), s32[]{:S(2)}) async-start(), calls=%async_computation.3 | async-start | bytes 8912896 | tf_op jit(solution)/shard_map/reduce_scatter | solution.py:76
  204.0 0.7 copy-start.3
  204.0 1.0 copy-start.1
  204.0 1.0 copy-start.2
  204.0 122.4 %copy-start.4 = (bf16[512,256]{1,0:T(8,128)(2,1)S(1)}, bf16[512,256]{1,0:T(8,128)(2,1)}, u32[]{:S(2)}) copy-start(bf16[512,256]{1,0:T(8,128)(2,1)} %param.16) | copy-start | bytes 786436
  204.0 290.0 %all-reduce.5.cloned.1.call-start = ((), (), s32[]{:S(2)}) async-start(), calls=%async_computation.6 | async-start | bytes 1048576 | tf_op jit(solution)/shard_map/psum | solution.py:16
  329.4 242.7 %all-gather.5.cloned.1.call-start = ((), (), s32[]{:S(2)}) async-start(), calls=%async_computation.4 | async-start | bytes 4456448 | tf_op jit(solution)/shard_map/all_gather | solution.py:22
  330.5 396.1 %all-reduce.7.cloned.1.call-start = ((), (), s32[]{:S(2)}) async-start(), calls=%async_computation.7 | async-start | bytes 1048576 | tf_op jit(solution)/shard_map/psum | solution.py:16
  494.1 332.9 %reduce-scatter.5.cloned.1.call-start = ((), (), s32[]{:S(2)}) async-start(), calls=%async_computation.5 | async-start | bytes 8912896 | tf_op jit(solution)/shard_map/reduce_scatter | solution.py:37
Sparse Core Ops, SparseCore 0:
  9.9 42.9 all-gather.2
  204.1 120.9 reduce-scatter.2
  329.6 164.4 all-reduce.4
  497.2 74.8 all-gather.4
  574.8 122.3 all-reduce.6
  726.7 100.2 reduce-scatter.4
